TPU v7x, 32 devices: a whole 2x2x4 slice. The times are simulated.
32 devices in a mesh: dp: 16 (over z, y, core), tensor: 2 (over x).
Axes of the slice: x: 2, y: 2, z: 4, core: 2. Of those that a mesh axis runs over, the one named last changes fastest.
Arguments:
- tokens: bfloat16 [81920, 1024], P(('dp', 'tensor')), may hold values from -6 to 6
- kept: int32 [256], P('dp'), may hold values from 180 to 256
- cotangent: bfloat16 [81920, 1024], P(('dp', 'tensor')), may hold values from -6 to 6
- w_qkv: bfloat16 [3, 1024, 1024], P(None, 'dp', 'tensor'), may hold values from -0.1875 to 0.1875
- w_out: bfloat16 [1024, 1024], P('tensor', 'dp'), may hold values from -0.75 to 0.75
- w_up: bfloat16 [1024, 4096], P('dp', 'tensor'), may hold values from -0.1875 to 0.1875
- w_down: bfloat16 [4096, 1024], P('tensor', 'dp'), may hold values from -0.09375 to 0.09375
- qv_bias: bfloat16 [2, 1024], P(None, ('tensor', 'dp')), may hold values from -3 to 3
- up_bias: bfloat16 [4096], P(('tensor', 'dp')), may hold values from -3 to 3
- ln_gain: float32 [2, 1024], P(None, ('dp', 'tensor')), may hold values from 0.5 to 1.5
- shift: float32 [4, 1024], P(None, ('dp', 'tensor')), may hold values from -3 to 3
Outputs:
- layer_out: bfloat16 [81920, 1024], P(('dp', 'tensor'))
- grad_tokens: float32 [81920, 1024], P(('dp', 'tensor'))
- grad_qkv: float32 [3, 1024, 1024], P(None, 'dp', 'tensor')
- grad_out: float32 [1024, 1024], P('tensor', 'dp')
- grad_up: float32 [1024, 4096], P('dp', 'tensor')
- grad_down: float32 [4096, 1024], P('tensor', 'dp')
- grad_qv_bias: float32 [2, 1024], P(None, ('tensor', 'dp'))
- grad_up_bias: float32 [4096], P(('tensor', 'dp'))
- grad_gain: float32 [2, 1024], P(None, ('dp', 'tensor'))
- grad_shift: float32 [4, 1024], P(None, ('dp', 'tensor'))
Inputs may be any that keep to these rules, and one draw needn't show every extreme that they name: kept patches of each image; an image's first 64 tokens and its first kept patch tokens are valid, the rest of its 320 tokens are padding.
All inputs are finite; a program needn't handle non-finite values.
Results may differ from a plain program's by a relative error of at most 0.02.
Values may be sent and summed in bfloat16 or wider, within the bound.
No kernel may reach another device: no remote copies, remote signals or barrier semaphores. Data moves between devices by JAX's collectives and lax.ppermute only.
A program may use at most 320 MiB of HBM per device.

v0:
```python
import jax
import jax.numpy as jnp
from jax import lax
from jax.sharding import PartitionSpec as P

HEAD_DIM = 64
BUFFER = 64
SEQ = 320
EPSILON = 1e-06
NEGATIVE = -1000000000.0


def times_flip(left, right):
    return lax.dot_general(
        left, right, (((1,), (1,)), ((), ())), preferred_element_type=jnp.float32
    )


def inner_rows(left, right):
    return lax.dot_general(
        left, right, (((0,), (0,)), ((), ())), preferred_element_type=jnp.float32
    )


def norm_parts(values):
    centred = values - jnp.mean(values, axis=-1, keepdims=True)
    inverse = lax.rsqrt(jnp.mean(centred * centred, axis=-1, keepdims=True) + EPSILON)
    return (centred * inverse, inverse)


def norm_back(grad_normed, normed, inverse):
    first = jnp.mean(grad_normed, axis=-1, keepdims=True)
    second = jnp.mean(grad_normed * normed, axis=-1, keepdims=True)
    return inverse * (grad_normed - first - normed * second)


def gelu_tanh(values):
    return jax.nn.gelu(values, approximate=True)


def fetch_params(w_qkv, w_out, w_up, w_down, qv_bias, up_bias):
    part_qkv, part_out, part_up, part_down, part_qv, part_bias = (
        lax.all_gather(w_qkv, "dp", axis=1, tiled=True),
        lax.all_gather(w_out, "dp", axis=1, tiled=True),
        lax.all_gather(w_up, "dp", axis=0, tiled=True),
        lax.all_gather(w_down, "dp", axis=1, tiled=True),
        lax.all_gather(qv_bias, "dp", axis=1, tiled=True),
        lax.all_gather(up_bias, "dp", axis=0, tiled=True),
    )
    return (part_qkv, part_out, part_up, part_down, part_qv, part_bias)


def narrow_mlp(grad_up, grad_down, grad_bias_up):
    return (grad_up, grad_down, grad_bias_up)


def narrow_attn(grad_qkv, grad_out, grad_qv_bias):
    return (grad_qkv, grad_out, grad_qv_bias)


def gather_acts(values):
    return lax.all_gather(values, "tensor", axis=0, tiled=True)


def gather_grads(values):
    return lax.all_gather(values, "tensor", axis=0, tiled=True)


def sum_forward(left, right, rows):

    def term(start, count):
        return jnp.dot(left, right, preferred_element_type=jnp.float32)

    return lax.psum_scatter(
        term(jnp.int32(0), rows * lax.axis_size("tensor")).astype(jnp.bfloat16),
        "tensor",
        scatter_dimension=0,
        tiled=True,
    ).astype(jnp.float32)


def sum_backward(lefts, rights, rows):

    def term(start, count):
        total = None
        for left, right in zip(lefts, rights):
            part = times_flip(left, right)
            total = part if total is None else total + part
        return total

    return lax.psum_scatter(
        term(jnp.int32(0), rows * lax.axis_size("tensor")),
        "tensor",
        scatter_dimension=0,
        tiled=True,
    )


def scores_of(query, key, keep):
    scores = jnp.einsum(
        "bqhe,bkhe->bhqk", query, key, preferred_element_type=jnp.float32
    ) * HEAD_DIM ** (-0.5)
    return jnp.where(keep[:, None, None, :] > 0.5, scores, NEGATIVE)


def attend(block):
    query, key, value, keep = block
    scores = scores_of(query, key, keep)
    highest = jnp.max(scores, axis=-1, keepdims=True)
    expo = jnp.exp(scores - highest)
    denom = jnp.sum(expo, axis=-1, keepdims=True)
    probs = (expo / denom).astype(jnp.bfloat16)
    result = jnp.einsum("bhqk,bkhe->bqhe", probs, value, preferred_element_type=jnp.float32)
    return (result.astype(jnp.bfloat16), (highest + jnp.log(denom))[..., 0])


def attend_back(block):
    query, key, value, keep, logsum, grad_attn = block
    scores = scores_of(query, key, keep)
    probs = jnp.exp(scores - logsum[..., None])
    grad_probs = jnp.einsum("bqhe,bkhe->bhqk", grad_attn, value, preferred_element_type=jnp.float32)
    grad_scores = probs * (grad_probs - jnp.sum(probs * grad_probs, axis=-1, keepdims=True))
    grad_scores = grad_scores.astype(jnp.bfloat16)
    scale = HEAD_DIM ** (-0.5)
    grad_query = (
        jnp.einsum("bhqk,bkhe->bqhe", grad_scores, key, preferred_element_type=jnp.float32) * scale
    )
    grad_key = (
        jnp.einsum("bhqk,bqhe->bkhe", grad_scores, query, preferred_element_type=jnp.float32)
        * scale
    )
    grad_value = jnp.einsum(
        "bhqk,bqhe->bkhe", probs.astype(jnp.bfloat16), grad_attn, preferred_element_type=jnp.float32
    )
    return (
        grad_query.astype(jnp.bfloat16),
        grad_key.astype(jnp.bfloat16),
        grad_value.astype(jnp.bfloat16),
    )


def body(tokens, kept, cotangent, w_qkv, w_out, w_up, w_down, qv_bias, up_bias, ln_gain, shift):
    rows = tokens.shape[0]
    full_qkv, full_out, full_up, full_down, bias_qv, bias_up = fetch_params(
        w_qkv, w_out, w_up, w_down, qv_bias, up_bias
    )
    gain, shifts = (
        lax.all_gather(ln_gain, ("dp", "tensor"), axis=1, tiled=True),
        lax.all_gather(shift, ("dp", "tensor"), axis=1, tiled=True),
    )
    heads = full_qkv.shape[2] // HEAD_DIM
    width = heads * HEAD_DIM
    positions = jnp.arange(SEQ, dtype=jnp.int32)
    images = kept.shape[0]
    keep = (positions[None, :] < BUFFER + kept[:, None]).astype(jnp.float32)
    group = images * SEQ
    offset = lax.axis_index("tensor") * rows
    keep_own = lax.dynamic_slice_in_dim(keep.reshape(group), offset, rows, 0)[:, None]
    pairs = images // 2
    keep_pairs = keep.reshape(pairs, 2, SEQ)
    x_values = tokens.astype(jnp.float32)
    normed1, inverse1 = norm_parts(x_values)
    h1_all = gather_acts((normed1 * gain[0] + shifts[0]).astype(jnp.bfloat16))
    bias_float = bias_qv.astype(jnp.float32)
    bias_rows = jnp.stack([bias_float[0], jnp.zeros_like(bias_float[0]), bias_float[1]])
    projected = jnp.einsum("rd,kdc->krc", h1_all, full_qkv, preferred_element_type=jnp.float32)
    qkv = (projected + bias_rows[:, None, :]).astype(jnp.bfloat16)
    split_shape = (pairs, 2, SEQ, heads, HEAD_DIM)
    query = qkv[0].reshape(split_shape)
    key = qkv[1].reshape(split_shape)
    value = qkv[2].reshape(split_shape)
    attn_blocks, logsum = lax.map(attend, (query, key, value, keep_pairs))
    attn = attn_blocks.reshape(group, width)
    mixed = x_values + sum_forward(attn, full_out, rows) + shifts[2]
    normed2, inverse2 = norm_parts(mixed)
    h2_all = gather_acts((normed2 * gain[1] + shifts[1]).astype(jnp.bfloat16))
    pre = jnp.dot(h2_all, full_up, preferred_element_type=jnp.float32) + bias_up.astype(jnp.float32)
    activated, gelu_pull = jax.vjp(gelu_tanh, pre)
    activated = activated.astype(jnp.bfloat16)
    result = (mixed + sum_forward(activated, full_down, rows) + shifts[3]) * keep_own
    layer_out = result.astype(jnp.bfloat16)
    full_qkv, full_out, full_up, full_down, spare_qv, spare_up = fetch_params(
        w_qkv, w_out, w_up, w_down, qv_bias, up_bias
    )
    grad = cotangent.astype(jnp.float32) * keep_own
    grad_m_all = gather_grads(grad.astype(jnp.bfloat16))
    grad_down = inner_rows(activated, grad_m_all)
    grad_pre = gelu_pull(times_flip(grad_m_all, full_down))[0].astype(jnp.bfloat16)
    grad_bias_up = jnp.sum(grad_pre, axis=0, dtype=jnp.float32)
    grad_up = inner_rows(h2_all, grad_pre)
    grad_up, grad_down, grad_bias_up = narrow_mlp(grad_up, grad_down, grad_bias_up)
    grad_h2 = sum_backward((grad_pre,), (full_up,), rows)
    grad_mixed = grad + norm_back(grad_h2 * gain[1], normed2, inverse2)
    grad_o_all = gather_grads(grad_mixed.astype(jnp.bfloat16))
    grad_out = inner_rows(attn, grad_o_all)
    grad_attn = times_flip(grad_o_all, full_out).astype(jnp.bfloat16).reshape(split_shape)
    grad_query, grad_key, grad_value = lax.map(
        attend_back, (query, key, value, keep_pairs, logsum, grad_attn)
    )
    grad_query = grad_query.reshape(group, width)
    grad_key = grad_key.reshape(group, width)
    grad_value = grad_value.reshape(group, width)
    stacked = jnp.stack([grad_query, grad_key, grad_value])
    grad_qkv = jnp.einsum("rd,krc->kdc", h1_all, stacked, preferred_element_type=jnp.float32)
    grad_qv_bias = jnp.stack(
        [
            jnp.sum(grad_query, axis=0, dtype=jnp.float32),
            jnp.sum(grad_value, axis=0, dtype=jnp.float32),
        ]
    )
    grad_h1 = sum_backward(
        (grad_query, grad_key, grad_value), (full_qkv[0], full_qkv[1], full_qkv[2]), rows
    )
    grad_tokens = grad_mixed + norm_back(grad_h1 * gain[0], normed1, inverse1)
    grad_qkv, grad_out, grad_qv_bias = narrow_attn(grad_qkv, grad_out, grad_qv_bias)
    sent_qkv, sent_out, sent_up, sent_down, sent_qv_bias, sent_bias_up = (
        lax.psum_scatter(
            grad_qkv.astype(jnp.bfloat16), "dp", scatter_dimension=1, tiled=True
        ).astype(jnp.float32),
        lax.psum_scatter(
            grad_out.astype(jnp.bfloat16), "dp", scatter_dimension=1, tiled=True
        ).astype(jnp.float32),
        lax.psum_scatter(
            grad_up.astype(jnp.bfloat16), "dp", scatter_dimension=0, tiled=True
        ).astype(jnp.float32),
        lax.psum_scatter(
            grad_down.astype(jnp.bfloat16), "dp", scatter_dimension=1, tiled=True
        ).astype(jnp.float32),
        lax.psum_scatter(
            grad_qv_bias.astype(jnp.bfloat16), "dp", scatter_dimension=1, tiled=True
        ).astype(jnp.float32),
        lax.psum_scatter(
            grad_bias_up.astype(jnp.bfloat16), "dp", scatter_dimension=0, tiled=True
        ).astype(jnp.float32),
    )
    grad_gain = jnp.stack([jnp.sum(grad_h1 * normed1, axis=0), jnp.sum(grad_h2 * normed2, axis=0)])
    grad_shift = jnp.stack(
        [
            jnp.sum(grad_h1, axis=0),
            jnp.sum(grad_h2, axis=0),
            jnp.sum(grad_mixed, axis=0),
            jnp.sum(grad, axis=0),
        ]
    )
    sent_gain, sent_shift = (
        lax.psum_scatter(grad_gain, ("dp", "tensor"), scatter_dimension=1, tiled=True),
        lax.psum_scatter(grad_shift, ("dp", "tensor"), scatter_dimension=1, tiled=True),
    )
    return (
        layer_out,
        grad_tokens,
        sent_qkv,
        sent_out,
        sent_up,
        sent_down,
        sent_qv_bias,
        sent_bias_up,
        sent_gain,
        sent_shift,
    )


def solution(mesh):
    return jax.shard_map(
        body,
        mesh=mesh,
        in_specs=(
            P(("dp", "tensor"), None),
            P("dp"),
            P(("dp", "tensor"), None),
            P(None, "dp", "tensor"),
            P("tensor", "dp"),
            P("dp", "tensor"),
            P("tensor", "dp"),
            P(None, ("tensor", "dp")),
            P(("tensor", "dp")),
            P(None, ("dp", "tensor")),
            P(None, ("dp", "tensor")),
        ),
        out_specs=(
            P(("dp", "tensor"), None),
            P(("dp", "tensor"), None),
            P(None, "dp", "tensor"),
            P("tensor", "dp"),
            P("dp", "tensor"),
            P("tensor", "dp"),
            P(None, ("tensor", "dp")),
            P(("tensor", "dp")),
            P(None, ("dp", "tensor")),
            P(None, ("dp", "tensor")),
        ),
        check_vma=False,
    )
```

profile of v0, /device:TPU:0, one launch (start us, length us, event | category | flops | bytes accessed | tf_op | source)
XLA Modules:
  0.0 2642.8 jit_solution(9621192983766315646)
XLA Ops:
  8.0 70.4 %all-gather = f32[32,32,2]{1,2,0:T(2,128)S(1)} all-gather(f32[1,32,2]{1,2,0:T(2,128)} %bitcast.235), channel_id=1, replica_groups=mesh['dp'=16,'tensor'=2] {'dp','tensor'}, dimensions={0}, use_global_device_ids=true | all-gather | bytes 8448 | tf_op jit(solution)/shard_map/all_gather | solution.py:148
  78.4 63.9 %all-gather.1 = f32[32,32,4]{1,2,0:T(4,128)S(1)} all-gather(f32[1,32,4]{1,2,0:T(4,128)} %bitcast.234), channel_id=1, replica_groups=mesh['dp'=16,'tensor'=2] {'dp','tensor'}, dimensions={0}, use_global_device_ids=true | all-gather | bytes 16896 | tf_op jit(solution)/shard_map/all_gather | solution.py:149
  154.2 17.3 all-gather.2
  171.8 108.7 %all-gather.13.cloned.1.call-done = bf16[5120,1024]{1,0:T(8,128)(2,1)} async-done(((bf16[2560,1024]{1,0:T(8,128)(2,1)}), bf16[5120,1024]{1,0:T(8,128)(2,1)}) %all-gather.13.cloned.1.call-update) | async-done | bytes 10485776 | tf_op jit(solution)/shard_map/all_gather | solution.py:62
  280.4 19.9 fusion.62
  306.3 13.9 reshape.173
  320.2 12.6 copy.101
  332.8 13.9 reshape.172
  346.7 12.7 copy.100
  359.3 13.9 reshape.171
  373.2 12.8 copy.99
  392.0 88.5 %while.26 = (s32[]{:T(128)}, bf16[8,2,320,8,64]{2,1,0,4,3:T(2,128)(2,1)}, f32[8,2,8,320]{3,2,1,0:T(8,128)}, bf16[8,2,320,8,64]{2,4,3,1,0:T(8,128)(2,1)}, f32[8,2...) while((s32[]{:T(128)}, ...), condition=%wide.region_5.6_spmd, body=%wide.region_2.5_spmd.sunk | while | flops 439414400 | bytes 24291436 | solution.py:172
  480.5 14.3 reshape.145
  506.8 121.5 %reduce-scatter.17.cloned.1.call-done = bf16[2560,1024]{1,0:T(8,128)(2,1)} async-done(((bf16[5120,1024]{1,0:T(8,128)(2,1)}), bf16[2560,1024]{1,0:T(8,128)(2,1)}) %reduce-scatter.17.cloned.1.call-update) | async-done | bytes 5242896 | tf_op jit(solution)/shard_map/reduce_scatter | solution.py:74
  651.4 21.7 all-gather.3
  680.9 130.0 %all-gather.19.cloned.1.call-done = bf16[5120,1024]{1,0:T(8,128)(2,1)} async-done(((bf16[2560,1024]{1,0:T(8,128)(2,1)}), bf16[5120,1024]{1,0:T(8,128)(2,1)}) %all-gather.19.cloned.1.call-update) | async-done | bytes 10485776 | tf_op jit(solution)/shard_map/all_gather | solution.py:62
  810.9 42.1 %multiply_convert_fusion.3 = (bf16[5120,2048]{1,0:T(8,128)(2,1)}, f32[5120,2048]{1,0:T(8,128)}) fusion(f32[2048]{0:T(1024)S(1)} %bitcast.232, bf16[5120,1024]{1,0:T(8,128)(2,1)} %all-gather.19.cloned.1.call-done, bf16[1024,2048]{1,0:T(8,128)(2,1)} %all-gather.21.cloned.1.call-done), kind=kOutput, calls=%fused_computation.71 | convolution fusion | flops 21579694080 | bytes 77602816 | tf_op jit(solution)/shard_map/dot_general | solution.py:177
  863.5 130.2 %all-gather.25.cloned.1.call-done = bf16[5120,1024]{1,0:T(8,128)(2,1)} async-done(((bf16[2560,1024]{1,0:T(8,128)(2,1)}), bf16[5120,1024]{1,0:T(8,128)(2,1)}) %all-gather.25.cloned.1.call-update) | async-done | bytes 10485776 | tf_op jit(solution)/shard_map/all_gather | solution.py:66
  993.6 56.0 %fusion.102 = (bf16[2048]{0:T(1024)(128)(2,1)}, bf16[5120,2048]{1,0:T(8,128)(2,1)}) fusion(f32[5120,2048]{1,0:T(8,128)} %get-tuple-element.277, f32[2048]{0:T(1024)S(1)} %bitcast.233, bf16[5120,1024]{1,0:T(8,128)(2,1)} %all-gather.25.cloned.1.call-done, bf16[2048,1024]{0,1:T(8,128)(2,1)} %all-gather.23.cloned.1.call-done), kind=kOutput, calls=%fused_computation.151 | convolution fusion | flops 21705521152 | bytes 77606912 | tf_op jit(solution)/shard_map/dot_general | solution.py:14
  1049.7 28.5 %fusion.103 = f32[5120,1024]{1,0:T(8,128)} fusion(bf16[5120,2048]{1,0:T(8,128)(2,1)} %get-tuple-element.279, bf16[1024,2048]{1,0:T(8,128)(2,1)} %all-gather.21.cloned.1.call-done), kind=kOutput, calls=%fused_computation.152 | convolution fusion | flops 21474836480 | bytes 46137344 | tf_op jit(solution)/shard_map/dot_general | solution.py:14
  1078.3 27.9 %convolution_convert_fusion.1 = bf16[5120,1024]{1,0:T(8,128)(2,1)} fusion(bf16[5120,2048]{1,0:T(8,128)(2,1)} %get-tuple-element.276, bf16[2048,1024]{0,1:T(8,128)(2,1)} %all-gather.23.cloned.1.call-done), kind=kOutput, calls=%fused_computation.112 | convolution fusion | flops 21480079360 | bytes 35651584 | tf_op jit(solution)/shard_map/dot_general | solution.py:72
  1106.2 206.4 %reduce-scatter.21.cloned.1.call-done = f32[2560,1024]{1,0:T(8,128)} async-done(((f32[5120,1024]{1,0:T(8,128)}), f32[2560,1024]{1,0:T(8,128)}) %reduce-scatter.21.cloned.1.call-update) | async-done | bytes 10485776 | tf_op jit(solution)/shard_map/reduce_scatter | solution.py:91
  1323.4 114.0 %reduce-scatter.19.cloned.1.call-done = bf16[2560,1024]{1,0:T(8,128)(2,1)} async-done(((bf16[5120,1024]{1,0:T(8,128)(2,1)}), bf16[2560,1024]{1,0:T(8,128)(2,1)}) %reduce-scatter.19.cloned.1.call-update) | async-done | bytes 5242896 | tf_op jit(solution)/shard_map/reduce_scatter | solution.py:74
  1437.4 16.5 fusion.97
  1461.2 29.1 %convolution_convert_fusion.3 = bf16[2048,1024]{0,1:T(8,128)(2,1)} fusion(bf16[5120,2048]{1,0:T(8,128)(2,1)} %get-tuple-element.276, bf16[5120,1024]{1,0:T(8,128)(2,1)} %all-gather.25.cloned.1.call-done), kind=kOutput, calls=%fused_computation.116 | convolution fusion | flops 21476933632 | bytes 35651584 | tf_op jit(solution)/shard_map/dot_general | solution.py:20
  1490.4 29.3 %convolution_convert_fusion.4 = bf16[1024,2048]{1,0:T(8,128)(2,1)} fusion(bf16[5120,1024]{1,0:T(8,128)(2,1)} %all-gather.19.cloned.1.call-done, bf16[5120,2048]{1,0:T(8,128)(2,1)} %get-tuple-element.279), kind=kOutput, calls=%fused_computation.117 | convolution fusion | flops 21476933632 | bytes 35651584 | tf_op jit(solution)/shard_map/dot_general | solution.py:20
  1519.8 71.1 %all-gather.27.cloned.1.call-done = bf16[5120,1024]{1,0:T(8,128)(2,1)} async-done(((bf16[2560,1024]{1,0:T(8,128)(2,1)}), bf16[5120,1024]{1,0:T(8,128)(2,1)}) %all-gather.27.cloned.1.call-update) | async-done | bytes 10485776 | tf_op jit(solution)/shard_map/all_gather | solution.py:66
  1602.1 14.0 reshape.162
  1616.1 12.7 copy.106
  1634.7 177.6 %while.27 = (s32[]{:T(128)}, bf16[8,2,320,8,64]{2,4,3,1,0:T(8,128)(2,1)}, bf16[8,2,320,8,64]{2,1,0,4,3:T(2,128)(2,1)}, bf16[8,2,320,8,64]{2,4,3,1,0:T(8,128)(2,1...) while((s32[]{:T(128)}, ...), condition=%wide.region_15.16_spmd, body=%wide.region_13.15_spmd.sunk | while | flops 1074785920 | bytes 58479748 | solution.py:197
  1812.3 12.7 copy.110
  1828.9 12.9 copy.108
  1846.6 14.3 stack_reshape.9
  1860.8 14.3 stack_reshape.11
  1875.1 14.3 stack_reshape.10
  1889.5 22.5 convert_bitcast_fusion
  1917.8 14.5 reshape.147
  1932.3 14.3 reshape.149
  1946.6 14.4 reshape.148
  1972.1 13.0 fusion.93
  1985.0 12.6 fusion.94
  1997.7 23.9 add_add_fusion
  2024.1 34.6 %all-reduce.1 = bf16[2048]{0:T(1024)(128)(2,1)S(1)} all-reduce(bf16[2048]{0:T(1024)(128)(2,1)S(1)} %copy-done.27), channel_id=11, replica_groups=mesh['dp'=16,'tensor'=2] {'dp'}, use_global_device_ids=true, to_apply=%region_27.28.clone | all-reduce | flops 2048 | bytes 8192
  2066.0 53.7 %reduce-scatter.25.cloned.1.call-done = bf16[512,64]{0,1:T(8,128)(2,1)} async-done(((bf16[512,1024]{0,1:T(8,128)(2,1)}), bf16[512,64]{0,1:T(8,128)(2,1)}) %reduce-scatter.25.cloned.1.call-update) | async-done | bytes 65552 | tf_op jit(solution)/shard_map/reduce_scatter | solution.py:220
  2121.3 233.9 %reduce-scatter.23.cloned.1.call-done = f32[2560,1024]{1,0:T(8,128)} async-done(((f32[5120,1024]{1,0:T(8,128)}), f32[2560,1024]{1,0:T(8,128)}) %reduce-scatter.23.cloned.1.call-update) | async-done | bytes 10485776 | tf_op jit(solution)/shard_map/reduce_scatter | solution.py:91
  2365.5 14.1 fusion.80
  2379.6 120.8 %reduce-scatter.33.cloned.1.call-done = f32[32,2]{1,0:T(8,128)} async-done(((f32[1024,2]{1,0:T(8,128)}), f32[32,2]{1,0:T(8,128)}) %reduce-scatter.33.cloned.1.call-update) | async-done | bytes 272
  2501.7 132.9 %reduce-scatter.35.cloned.1.call-done = f32[32,4]{1,0:T(8,128)} async-done(((f32[1024,4]{1,0:T(8,128)}), f32[32,4]{1,0:T(8,128)}) %reduce-scatter.35.cloned.1.call-update) | async-done | bytes 528
  (307 shorter events, 427.2 us)
Async XLA Ops:
  7.2 164.6 %all-gather.15.cloned.1.call-start = ((), (), s32[]{:S(2)}) async-start(), calls=%async_computation.11 | async-start | bytes 3342336 | tf_op jit(solution)/shard_map/all_gather | solution.py:43
  7.9 272.5 %all-gather.13.cloned.1.call-start = ((), (), s32[]{:S(2)}) async-start(), calls=%async_computation.10 | async-start | bytes 15728640 | tf_op jit(solution)/shard_map/all_gather | solution.py:62
  142.5 4.2 copy-start
  143.1 5.8 copy-start.17
  148.2 5.5 copy-start.33
  148.2 6.0 copy-start.30
  152.8 341.9 %all-gather.17.cloned.1.call-start = ((), (), s32[]{:S(2)}) async-start(), calls=%async_computation.12 | async-start | bytes 1114112 | tf_op jit(solution)/shard_map/all_gather | solution.py:44
  153.6 474.7 %reduce-scatter.17.cloned.1.call-start = ((), (), s32[]{:S(2)}) async-start(), calls=%async_computation.13 | async-start | bytes 15728640 | tf_op jit(solution)/shard_map/reduce_scatter | solution.py:74
  480.4 25.7 copy-start.14
  506.1 122.1 %copy-start.12 = (f32[1,1024]{1,0:T(1,128)S(1)}, f32[1,1024]{1,0:T(1,128)}, u32[]{:S(2)}) copy-start(f32[1,1024]{1,0:T(1,128)} %get-tuple-element.270) | copy-start | bytes 12292
  506.1 128.1 %slice-start = ((s8[5242880]{0:T(1024)(128)(4,1)}), s8[1048576]{0:T(1024)(128)(4,1)S(1)}, s32[]{:S(2)}) async-start(s8[5242880]{0:T(1024)(128)(4,1)} %bitcast.201), calls=%async_computation.29 | async-start | bytes 2097152
  506.2 174.7 %all-gather.21.cloned.1.call-start = ((), (), s32[]{:S(2)}) async-start(), calls=%async_computation.15 | async-start | bytes 4456448 | tf_op jit(solution)/shard_map/all_gather | solution.py:45
  506.7 304.1 %all-gather.19.cloned.1.call-start = ((), (), s32[]{:S(2)}) async-start(), calls=%async_computation.14 | async-start | bytes 15728640 | tf_op jit(solution)/shard_map/all_gather | solution.py:62
  628.2 6.0 copy-start.1
  628.2 6.8 slice-start.1
  628.3 11.0 copy-start.19
  628.3 11.0 copy-start.23
  639.2 5.5 copy-start.29
  643.9 7.5 copy-start.31
  643.9 219.6 %all-gather.23.cloned.1.call-start = ((), (), s32[]{:S(2)}) async-start(), calls=%async_computation.16 | async-start | bytes 4456448 | tf_op jit(solution)/shard_map/all_gather | solution.py:46
  644.6 349.0 %all-gather.25.cloned.1.call-start = ((), (), s32[]{:S(2)}) async-start(), calls=%async_computation.18 | async-start | bytes 15728640 | tf_op jit(solution)/shard_map/all_gather | solution.py:66
  651.3 661.4 %reduce-scatter.21.cloned.1.call-start = ((), (), s32[]{:S(2)}) async-start(), calls=%async_computation.19 | async-start | bytes 31457280 | tf_op jit(solution)/shard_map/reduce_scatter | solution.py:91
  1078.2 359.2 %reduce-scatter.19.cloned.1.call-start = ((), (), s32[]{:S(2)}) async-start(), calls=%async_computation.17 | async-start | bytes 15728640 | tf_op jit(solution)/shard_map/reduce_scatter | solution.py:74
  1106.1 206.6 %copy-start.7 = (f32[2560]{0:T(1024)S(1)}, f32[2560]{0:T(1024)}, u32[]{:S(2)}) copy-start(f32[2560]{0:T(1024)} %copy-done.6) | copy-start | bytes 30724
  1106.1 206.6 %copy-start.11 = (f32[2560]{0:T(1024)S(1)}, f32[2560]{0:T(1024)}, u32[]{:S(2)}) copy-start(f32[2560]{0:T(1024)} %copy-done.10) | copy-start | bytes 30724
  1106.1 206.6 %copy-start.13 = (f32[1,1024]{1,0:T(1,128)S(1)}, f32[1,1024]{1,0:T(1,128)}, u32[]{:S(2)}) copy-start(f32[1,1024]{1,0:T(1,128)} %get-tuple-element.270) | copy-start | bytes 12292
  1106.1 206.6 %copy-start.20 = (f32[1,1024]{1,0:T(1,128)S(1)}, f32[1,1024]{1,0:T(1,128)}, u32[]{:S(2)}) copy-start(f32[1,1024]{1,0:T(1,128)} %get-tuple-element.273) | copy-start | bytes 12292
  1106.2 331.2 %copy-start.16 = (f32[2560]{0:T(1024)S(1)}, f32[2560]{0:T(1024)}, u32[]{:S(2)}) copy-start(f32[2560]{0:T(1024)} %copy-done.15) | copy-start | bytes 30724
  1106.2 331.2 %copy-start.26 = (f32[1,1024]{1,0:T(1,128)S(1)}, f32[1,1024]{1,0:T(1,128)}, u32[]{:S(2)}) copy-start(f32[1,1024]{1,0:T(1,128)} %get-tuple-element.268) | copy-start | bytes 12292
  1106.2 484.6 %all-gather.27.cloned.1.call-start = ((), (), s32[]{:S(2)}) async-start(), calls=%async_computation.20 | async-start | bytes 15728640 | tf_op jit(solution)/shard_map/all_gather | solution.py:66
  1453.9 4.1 copy-start.2
  1461.2 598.1 %reduce-scatter.29.cloned.1.call-start = ((), (), s32[]{:S(2)}) async-start(), calls=%async_computation.24 | async-start | bytes 4456448 | tf_op jit(solution)/shard_map/reduce_scatter | solution.py:226
  1490.3 570.7 %reduce-scatter.27.cloned.1.call-start = ((), (), s32[]{:S(2)}) async-start(), calls=%async_computation.23 | async-start | bytes 4456448 | tf_op jit(solution)/shard_map/reduce_scatter | solution.py:223
  1490.4 100.4 %copy-start.32 = (bf16[512,1024]{0,1:T(8,128)(2,1)S(1)}, bf16[512,1024]{0,1:T(8,128)(2,1)}, u32[]{:S(2)}) copy-start(bf16[512,1024]{0,1:T(8,128)(2,1)} %all-gather.17.cloned.1.call-done) | copy-start | bytes 3145732
  1519.7 543.1 %reduce-scatter.31.cloned.1.call-start = ((), (), s32[]{:S(2)}) async-start(), calls=%async_computation.25 | async-start | bytes 139264
  1889.5 174.7 %all-reduce.4.cloned.1.call-start = ((), (), s32[]{:S(2)}) async-start(), calls=%async_computation.28 | async-start | bytes 8388608
  1917.8 202.0 %reduce-scatter.25.cloned.1.call-start = ((), (), s32[]{:S(2)}) async-start(), calls=%async_computation.22 | async-start | bytes 1114112 | tf_op jit(solution)/shard_map/reduce_scatter | solution.py:220
  1961.0 11.0 copy-start.3
  1972.0 383.2 %reduce-scatter.23.cloned.1.call-start = ((), (), s32[]{:S(2)}) async-start(), calls=%async_computation.21 | async-start | bytes 31457280 | tf_op jit(solution)/shard_map/reduce_scatter | solution.py:91
  2021.6 333.7 %copy-start.5 = (f32[2560]{0:T(1024)S(1)}, f32[2560]{0:T(1024)}, u32[]{:S(2)}) copy-start(f32[2560]{0:T(1024)} %copy-done.4) | copy-start | bytes 30724
  2021.6 333.7 %copy-start.9 = (f32[2560]{0:T(1024)S(1)}, f32[2560]{0:T(1024)}, u32[]{:S(2)}) copy-start(f32[2560]{0:T(1024)} %copy-done.8) | copy-start | bytes 30724
  2021.6 333.7 %copy-start.18 = (f32[1,1024]{1,0:T(1,128)S(1)}, f32[1,1024]{1,0:T(1,128)}, u32[]{:S(2)}) copy-start(f32[1,1024]{1,0:T(1,128)} %copy-done.17) | copy-start | bytes 12292
  2021.6 478.8 %reduce-scatter.33.cloned.1.call-start = ((), (), s32[]{:S(2)}) async-start(), calls=%async_computation.26 | async-start | bytes 540672
  2065.2 298.1 %copy-start.21 = (f32[1024]{0:T(1024)S(1)}, f32[1024]{0:T(1024)}, u32[]{:S(2)}) copy-start(f32[1024]{0:T(1024)} %get-tuple-element.215) | copy-start | bytes 12292
  2121.3 243.1 %copy-start.22 = (f32[1024]{0:T(1024)S(1)}, f32[1024]{0:T(1024)}, u32[]{:S(2)}) copy-start(f32[1024]{0:T(1024)} %get-tuple-element.222) | copy-start | bytes 12292
  2121.3 243.1 %copy-start.24 = (f32[1024]{0:T(1024)S(1)}, f32[1024]{0:T(1024)}, u32[]{:S(2)}) copy-start(f32[1024]{0:T(1024)} %get-tuple-element.257) | copy-start | bytes 12292
  2121.3 243.1 %copy-start.25 = (f32[1024]{0:T(1024)S(1)}, f32[1024]{0:T(1024)}, u32[]{:S(2)}) copy-start(f32[1024]{0:T(1024)} %get-tuple-element.267) | copy-start | bytes 12292
  2364.4 270.3 %reduce-scatter.35.cloned.1.call-start = ((), (), s32[]{:S(2)}) async-start(), calls=%async_computation.27 | async-start | bytes 540672
  (8 other events, 11.3 us)
Sparse Core Ops, SparseCore 0:
  10.2 48.2 all-gather.14
  153.0 127.4 all-gather.12
  282.6 37.8 all-gather.16
  506.3 121.9 reduce-scatter.16
  630.3 50.5 all-gather.20
  682.9 127.9 all-gather.18
  813.0 50.3 all-gather.22
  865.6 127.9 all-gather.24
  1078.3 234.2 reduce-scatter.20
  1315.4 121.9 reduce-scatter.18
  1461.3 129.4 all-gather.26
  1594.5 72.7 reduce-scatter.28
  1671.2 71.8 reduce-scatter.26
  1889.6 55.8 reduce-scatter.30
  1949.0 110.3 all-reduce.3
  2062.8 56.9 reduce-scatter.24
  2121.9 233.2 reduce-scatter.22
  2364.5 135.8 reduce-scatter.32
  2502.6 131.9 reduce-scatter.34
where the time goes:
time: 2650 us; the launch traced here: 2640 us
  waiting for transfers between devices  1440 us (54%)
  matrix products  525 us (20%)
  local copies, waits for them, and re-layouts  306 us (12%)
  blocking collectives  208 us (8%)
  other arithmetic  142 us (5%)
    reduce_scatter x2, waiting for transfers between devices, sum_backward(): lax.psum_scatter(term(jnp.int32(0), rows * lax.axis_size('tensor')), 'ten...  440 us
    unnamed x23, waiting for transfers between devices  257 us
    all_gather x2, waiting for transfers between devices, gather_acts(): return lax.all_gather(values, 'tensor', axis=0, tiled=True)  239 us
    reduce_scatter x2, waiting for transfers between devices, sum_forward(): lax.psum_scatter(term(jnp.int32(0), rows * lax.axis_size('tensor')).astyp...  235 us
    all_gather x2, waiting for transfers between devices, gather_grads(): return lax.all_gather(values, 'tensor', axis=0, tiled=True)  201 us
    dot_general x6, matrix products, times_flip(): lax.dot_general(left, right, (((1,), (1,)), ((), ())), preferred_element_...  145 us
    all_gather x1, blocking collectives, body(): lax.all_gather(ln_gain, ('dp', 'tensor'), axis=1, tiled=True)  70.4 us
    dot_general x3, matrix products, inner_rows(): lax.dot_general(left, right, (((0,), (0,)), ((), ())), preferred_element_...  69.3 us
  transfers between devices with their start and end apart: 19, of which 13 were waited for; matrix products, arithmetic and copies ran while one was open for 32% of the time, Pallas kernels for 0%

commit v1 on v0

--- a/solution.py
+++ b/solution.py
@@ -8,6 +8,13 @@
 SEQ = 320
 EPSILON = 1e-06
 NEGATIVE = -1000000000.0
+
+
+def swapped_in(array, mesh_axis, d):
+    size = lax.axis_size(mesh_axis)
+    tiles = jnp.stack([array for _ in range(size)])
+    tiles = lax.all_to_all(tiles, mesh_axis, split_axis=0, concat_axis=0)
+    return jnp.concatenate(tiles, axis=d)
 
 
 def times_flip(left, right):
@@ -59,7 +66,7 @@
 
 
 def gather_acts(values):
-    return lax.all_gather(values, "tensor", axis=0, tiled=True)
+    return swapped_in(values, "tensor", 0)
 
 
 def gather_grads(values):

time: 2650 us -> 2550 us (0.962)
  waiting for transfers between devices: 1440 us -> 1300 us
    all_gather x2 -> x0, waiting for transfers between devices: 239 us -> none  [gather_acts(): return lax.all_gather(values, 'tensor', axis=0, tiled=True)]
    all_to_all x0 -> x2, waiting for transfers between devices: none -> 209 us  [swapped_in(): tiles = lax.all_to_all(tiles, mesh_axis, split_axis=0, concat_axis=0)]
    all_gather x2, waiting for transfers between devices: 201 us -> 113 us  [gather_grads(): return lax.all_gather(values, 'tensor', axis=0, tiled=True)]
    another operation x2 -> x6, other arithmetic: 0.01 us -> 29.7 us  [the longest x4 29.7 us: swapped_in(): tiles = jnp.stack([array for _ in range(size)])]
    unnamed x23 -> x21, waiting for transfers between devices: 257 us -> 256 us
  transfers between devices with their start and end apart: 19 -> 19, of which waited for: 13 -> 11; matrix products, arithmetic and copies ran while one was open for 32% -> 34% of each run, Pallas kernels for 0% -> 0%
where the time goes in v1:
time: 2550 us; the launch traced here: 2540 us
  waiting for transfers between devices  1300 us (51%)
  matrix products  525 us (21%)
  local copies, waits for them, and re-layouts  306 us (12%)
  blocking collectives  207 us (8%)
  other arithmetic  165 us (6%)
    reduce_scatter x2, waiting for transfers between devices, sum_backward(): lax.psum_scatter(term(jnp.int32(0), rows * lax.axis_size('tensor')), 'ten...  440 us
    unnamed x21, waiting for transfers between devices  256 us
    reduce_scatter x2, waiting for transfers between devices, sum_forward(): lax.psum_scatter(term(jnp.int32(0), rows * lax.axis_size('tensor')).astyp...  231 us
    all_to_all x2, waiting for transfers between devices, swapped_in(): tiles = lax.all_to_all(tiles, mesh_axis, split_axis=0, concat_axis=0)  209 us
    dot_general x6, matrix products, times_flip(): lax.dot_general(left, right, (((1,), (1,)), ((), ())), preferred_element_...  145 us
    all_gather x2, waiting for transfers between devices, gather_grads(): return lax.all_gather(values, 'tensor', axis=0, tiled=True)  113 us
    all_gather x1, blocking collectives, body(): lax.all_gather(ln_gain, ('dp', 'tensor'), axis=1, tiled=True)  70.1 us
    dot_general x3, matrix products, inner_rows(): lax.dot_general(left, right, (((0,), (0,)), ((), ())), preferred_element_...  69.3 us
  transfers between devices with their start and end apart: 19, of which 11 were waited for; matrix products, arithmetic and copies ran while one was open for 34% of the time, Pallas kernels for 0%

profile of v1, /device:TPU:0, one launch (start us, length us, event | category | flops | bytes accessed | tf_op | source)
XLA Modules:
  0.0 2538.8 jit_solution(4083613759570185385)
XLA Ops:
  15.2 70.1 %all-gather = f32[32,32,2]{1,2,0:T(2,128)S(1)} all-gather(f32[1,32,2]{1,2,0:T(2,128)S(1)} %bitcast.238), channel_id=1, replica_groups=mesh['dp'=16,'tensor'=2] {'dp','tensor'}, dimensions={0}, use_global_device_ids=true | all-gather | bytes 8448 | tf_op jit(solution)/shard_map/all_gather | solution.py:155
  85.5 63.7 %all-gather.1 = f32[32,32,4]{1,2,0:T(4,128)S(1)} all-gather(f32[1,32,4]{1,2,0:T(4,128)S(1)} %bitcast.237), channel_id=1, replica_groups=mesh['dp'=16,'tensor'=2] {'dp','tensor'}, dimensions={0}, use_global_device_ids=true | all-gather | bytes 16896 | tf_op jit(solution)/shard_map/all_gather | solution.py:156
  175.5 17.6 all-gather.2
  193.4 93.3 %all-to-all-done = bf16[2,2560,1024]{2,1,0:T(8,128)(2,1)} async-done(((bf16[2,2560,1024]{2,1,0:T(8,128)(2,1)}), bf16[2,2560,1024]{2,1,0:T(8,128)(2,1)}, u32[]{:S(2)}, u32[]{:S(2)}) %all-to-all-start) | async-done | bytes 10485792 | tf_op jit(solution)/shard_map/all_to_all | solution.py:16
  286.8 19.9 fusion.62
  312.6 13.9 reshape.181
  326.5 12.6 copy.101
  339.1 13.9 reshape.180
  352.9 12.6 copy.100
  365.5 13.9 reshape.179
  379.4 12.8 copy.99
  398.1 88.5 %while.26 = (s32[]{:T(128)}, bf16[8,2,320,8,64]{2,1,0,4,3:T(2,128)(2,1)}, f32[8,2,8,320]{3,2,1,0:T(8,128)}, bf16[8,2,320,8,64]{2,4,3,1,0:T(8,128)(2,1)}, f32[8,2...) while((s32[]{:T(128)}, ...), condition=%wide.region_5.6_spmd, body=%wide.region_2.5_spmd.sunk | while | flops 439414400 | bytes 24291436 | solution.py:179
  486.6 14.3 reshape.152
  513.5 116.7 %reduce-scatter.17.cloned.1.call-done = bf16[2560,1024]{1,0:T(8,128)(2,1)} async-done(((bf16[5120,1024]{1,0:T(8,128)(2,1)}), bf16[2560,1024]{1,0:T(8,128)(2,1)}) %reduce-scatter.17.cloned.1.call-update) | async-done | bytes 5242896 | tf_op jit(solution)/shard_map/reduce_scatter | solution.py:81
  668.9 21.3 all-gather.3
  690.2 115.4 %all-to-all-done.1 = bf16[2,2560,1024]{2,1,0:T(8,128)(2,1)} async-done(((bf16[2,2560,1024]{2,1,0:T(8,128)(2,1)}), bf16[2,2560,1024]{2,1,0:T(8,128)(2,1)}, u32[]{:S(2)}, u32[]{:S(2)}) %all-to-all-start.1) | async-done | bytes 10485792 | tf_op jit(solution)/shard_map/all_to_all | solution.py:16
  805.6 42.3 %multiply_convert_fusion.3 = (bf16[5120,2048]{1,0:T(8,128)(2,1)}, f32[5120,2048]{1,0:T(8,128)}) fusion(f32[2048]{0:T(1024)S(1)} %bitcast.235, bf16[5120,1024]{1,0:T(8,128)(2,1)} %bitcast.38, bf16[1024,2048]{1,0:T(8,128)(2,1)} %all-gather.15.cloned.1.call-done), kind=kOutput, calls=%fused_computation.71 | convolution fusion | flops 21579694080 | bytes 77602816 | tf_op jit(solution)/shard_map/dot_general | solution.py:184
  847.9 42.4 %all-gather.19.cloned.1.call-done = bf16[5120,1024]{1,0:T(8,128)(2,1)} async-done(((bf16[2560,1024]{1,0:T(8,128)(2,1)}), bf16[5120,1024]{1,0:T(8,128)(2,1)}) %all-gather.19.cloned.1.call-update) | async-done | bytes 10485776 | tf_op jit(solution)/shard_map/all_gather | solution.py:73
  890.2 56.0 %fusion.100 = (bf16[2048]{0:T(1024)(128)(2,1)}, bf16[5120,2048]{1,0:T(8,128)(2,1)}) fusion(f32[5120,2048]{1,0:T(8,128)} %get-tuple-element.277, f32[2048]{0:T(1024)S(1)} %bitcast.236, bf16[5120,1024]{1,0:T(8,128)(2,1)} %all-gather.19.cloned.1.call-done, bf16[2048,1024]{0,1:T(8,128)(2,1)} %all-gather.17.cloned.1.call-done), kind=kOutput, calls=%fused_computation.153 | convolution fusion | flops 21705521152 | bytes 77606912 | tf_op jit(solution)/shard_map/dot_general | solution.py:21
  946.2 28.3 %fusion.101 = f32[5120,1024]{1,0:T(8,128)} fusion(bf16[5120,2048]{1,0:T(8,128)(2,1)} %get-tuple-element.279, bf16[1024,2048]{1,0:T(8,128)(2,1)} %all-gather.15.cloned.1.call-done), kind=kOutput, calls=%fused_computation.154 | convolution fusion | flops 21474836480 | bytes 46137344 | tf_op jit(solution)/shard_map/dot_general | solution.py:21
  974.5 27.8 %convolution_convert_fusion.1 = bf16[5120,1024]{1,0:T(8,128)(2,1)} fusion(bf16[5120,2048]{1,0:T(8,128)(2,1)} %get-tuple-element.276, bf16[2048,1024]{0,1:T(8,128)(2,1)} %all-gather.17.cloned.1.call-done), kind=kOutput, calls=%fused_computation.112 | convolution fusion | flops 21480079360 | bytes 35651584 | tf_op jit(solution)/shard_map/dot_general | solution.py:79
  1002.5 206.4 %reduce-scatter.21.cloned.1.call-done = f32[2560,1024]{1,0:T(8,128)} async-done(((f32[5120,1024]{1,0:T(8,128)}), f32[2560,1024]{1,0:T(8,128)}) %reduce-scatter.21.cloned.1.call-update) | async-done | bytes 10485776 | tf_op jit(solution)/shard_map/reduce_scatter | solution.py:98
  1219.9 113.9 %reduce-scatter.19.cloned.1.call-done = bf16[2560,1024]{1,0:T(8,128)(2,1)} async-done(((bf16[5120,1024]{1,0:T(8,128)(2,1)}), bf16[2560,1024]{1,0:T(8,128)(2,1)}) %reduce-scatter.19.cloned.1.call-update) | async-done | bytes 5242896 | tf_op jit(solution)/shard_map/reduce_scatter | solution.py:81
  1333.8 16.5 fusion.95
  1357.6 29.1 %convolution_convert_fusion.3 = bf16[2048,1024]{0,1:T(8,128)(2,1)} fusion(bf16[5120,2048]{1,0:T(8,128)(2,1)} %get-tuple-element.276, bf16[5120,1024]{1,0:T(8,128)(2,1)} %all-gather.19.cloned.1.call-done), kind=kOutput, calls=%fused_computation.118 | convolution fusion | flops 21476933632 | bytes 35651584 | tf_op jit(solution)/shard_map/dot_general | solution.py:27
  1386.8 29.3 %convolution_convert_fusion.4 = bf16[1024,2048]{1,0:T(8,128)(2,1)} fusion(bf16[5120,1024]{1,0:T(8,128)(2,1)} %bitcast.38, bf16[5120,2048]{1,0:T(8,128)(2,1)} %get-tuple-element.279), kind=kOutput, calls=%fused_computation.119 | convolution fusion | flops 21476933632 | bytes 35651584 | tf_op jit(solution)/shard_map/dot_general | solution.py:27
  1416.2 71.0 %all-gather.21.cloned.1.call-done = bf16[5120,1024]{1,0:T(8,128)(2,1)} async-done(((bf16[2560,1024]{1,0:T(8,128)(2,1)}), bf16[5120,1024]{1,0:T(8,128)(2,1)}) %all-gather.21.cloned.1.call-update) | async-done | bytes 10485776 | tf_op jit(solution)/shard_map/all_gather | solution.py:73
  1498.5 14.0 reshape.170
  1512.6 12.6 copy.106
  1531.0 177.5 %while.27 = (s32[]{:T(128)}, bf16[8,2,320,8,64]{2,4,3,1,0:T(8,128)(2,1)}, bf16[8,2,320,8,64]{2,1,0,4,3:T(2,128)(2,1)}, bf16[8,2,320,8,64]{2,4,3,1,0:T(8,128)(2,1...) while((s32[]{:T(128)}, ...), condition=%wide.region_15.16_spmd, body=%wide.region_13.15_spmd.sunk | while | flops 1074785920 | bytes 58479748 | solution.py:204
  1708.5 12.7 copy.110
  1725.1 13.1 copy.108
  1742.9 14.3 stack_reshape.9
  1757.2 14.3 stack_reshape.11
  1771.5 14.3 stack_reshape.10
  1785.9 22.5 convert_bitcast_fusion
  1814.2 14.5 reshape.155
  1828.7 14.3 reshape.157
  1843.0 14.3 reshape.156
  1868.3 12.9 fusion.91
  1881.2 12.7 fusion.92
  1893.9 23.9 add_add_fusion
  1920.3 34.7 %all-reduce.1 = bf16[2048]{0:T(1024)(128)(2,1)S(1)} all-reduce(bf16[2048]{0:T(1024)(128)(2,1)S(1)} %copy-done.26), channel_id=11, replica_groups=mesh['dp'=16,'tensor'=2] {'dp'}, use_global_device_ids=true, to_apply=%region_27.28.clone | all-reduce | flops 2048 | bytes 8192
  1962.4 53.9 %reduce-scatter.25.cloned.1.call-done = bf16[512,64]{0,1:T(8,128)(2,1)} async-done(((bf16[512,1024]{0,1:T(8,128)(2,1)}), bf16[512,64]{0,1:T(8,128)(2,1)}) %reduce-scatter.25.cloned.1.call-update) | async-done | bytes 65552 | tf_op jit(solution)/shard_map/reduce_scatter | solution.py:227
  2017.8 234.0 %reduce-scatter.23.cloned.1.call-done = f32[2560,1024]{1,0:T(8,128)} async-done(((f32[5120,1024]{1,0:T(8,128)}), f32[2560,1024]{1,0:T(8,128)}) %reduce-scatter.23.cloned.1.call-update) | async-done | bytes 10485776 | tf_op jit(solution)/shard_map/reduce_scatter | solution.py:98
  2262.1 14.1 fusion.80
  2276.2 120.6 %reduce-scatter.33.cloned.1.call-done = f32[32,2]{1,0:T(8,128)} async-done(((f32[1024,2]{1,0:T(8,128)}), f32[32,2]{1,0:T(8,128)}) %reduce-scatter.33.cloned.1.call-update) | async-done | bytes 272
  2398.2 132.5 %reduce-scatter.35.cloned.1.call-done = f32[32,4]{1,0:T(8,128)} async-done(((f32[1024,4]{1,0:T(8,128)}), f32[32,4]{1,0:T(8,128)}) %reduce-scatter.35.cloned.1.call-update) | async-done | bytes 528
  (309 shorter events, 447.1 us)
Async XLA Ops:
  7.2 8.0 copy-start.30
  7.2 78.3 %copy-start.27 = (f32[4,32]{1,0:T(4,128)S(1)}, f32[4,32]{1,0:T(4,128)}, u32[]{:S(2)}) copy-start(f32[4,32]{1,0:T(4,128)} %param.25) | copy-start | bytes 1540
  7.2 279.6 %all-gather.11.cloned.1.call-start = ((), (), s32[]{:S(2)}) async-start(), calls=%async_computation.12 | async-start | bytes 3342336 | tf_op jit(solution)/shard_map/all_gather | solution.py:50
  11.2 155.2 %copy-start.3 = (f32[2560]{0:T(1024)}, f32[2560]{0:T(1024)S(1)}, u32[]{:S(2)}) copy-start(f32[2560]{0:T(1024)S(1)} %broadcast_multiply_fusion.5) | copy-start | bytes 30724
  15.2 151.2 %copy-start.7 = (f32[2560]{0:T(1024)}, f32[2560]{0:T(1024)S(1)}, u32[]{:S(2)}) copy-start(f32[2560]{0:T(1024)S(1)} %add_rsqrt_fusion.1) | copy-start | bytes 30724
  150.4 16.0 copy-start.16
  166.4 8.6 copy-start.34
  166.4 9.1 copy-start.31
  166.5 120.3 %all-to-all-start = ((bf16[2,2560,1024]{2,1,0:T(8,128)(2,1)}), bf16[2,2560,1024]{2,1,0:T(8,128)(2,1)}, u32[]{:S(2)}, u32[]{:S(2)}) async-start(bf16[2,2560,1024]{2,1,0:T(8,128)(2,1)} %pad_maximum_fusion), calls=%async_computation | async-start | bytes 20971520 | tf_op jit(solution)/shard_map/all_to_all | solution.py:16
  174.2 326.8 %all-gather.13.cloned.1.call-start = ((), (), s32[]{:S(2)}) async-start(), calls=%async_computation.13 | async-start | bytes 1114112 | tf_op jit(solution)/shard_map/all_gather | solution.py:51
  174.9 455.4 %reduce-scatter.17.cloned.1.call-start = ((), (), s32[]{:S(2)}) async-start(), calls=%async_computation.14 | async-start | bytes 15728640 | tf_op jit(solution)/shard_map/reduce_scatter | solution.py:81
  486.6 25.5 %copy-start.13 = (f32[8,2,320]{2,1,0:T(2,128)}, f32[8,2,320]{2,1,0:T(2,128)S(1)}, u32[]{:S(2)}) copy-start(f32[8,2,320]{2,1,0:T(2,128)S(1)} %get-tuple-element.514) | copy-start | bytes 61444
  512.1 118.2 %copy-start.11 = (f32[1,1024]{1,0:T(1,128)S(1)}, f32[1,1024]{1,0:T(1,128)}, u32[]{:S(2)}) copy-start(f32[1,1024]{1,0:T(1,128)} %get-tuple-element.270) | copy-start | bytes 12292
  512.1 124.2 %slice-start = ((s8[5242880]{0:T(1024)(128)(4,1)}), s8[1048576]{0:T(1024)(128)(4,1)S(1)}, s32[]{:S(2)}) async-start(s8[5242880]{0:T(1024)(128)(4,1)} %bitcast.204), calls=%async_computation.29 | async-start | bytes 2097152
  512.1 178.0 %all-gather.15.cloned.1.call-start = ((), (), s32[]{:S(2)}) async-start(), calls=%async_computation.15 | async-start | bytes 4456448 | tf_op jit(solution)/shard_map/all_gather | solution.py:52
  512.7 335.1 %all-gather.17.cloned.1.call-start = ((), (), s32[]{:S(2)}) async-start(), calls=%async_computation.16 | async-start | bytes 4456448 | tf_op jit(solution)/shard_map/all_gather | solution.py:53
  513.5 149.4 %copy-start.14 = (f32[2560]{0:T(1024)}, f32[2560]{0:T(1024)S(1)}, u32[]{:S(2)}) copy-start(f32[2560]{0:T(1024)S(1)} %dynamic_slice.36) | copy-start | bytes 30724
  630.3 6.8 slice-start.1
  630.3 11.0 copy-start.18
  630.3 11.0 copy-start.22
  655.0 150.6 %all-to-all-start.1 = ((bf16[2,2560,1024]{2,1,0:T(8,128)(2,1)}), bf16[2,2560,1024]{2,1,0:T(8,128)(2,1)}, u32[]{:S(2)}, u32[]{:S(2)}) async-start(bf16[2,2560,1024]{2,1,0:T(8,128)(2,1)} %pad_maximum_fusion.1), calls=%async_computation.2 | async-start | bytes 20971520 | tf_op jit(solution)/shard_map/all_to_all | solution.py:16
  662.9 227.3 %all-gather.19.cloned.1.call-start = ((), (), s32[]{:S(2)}) async-start(), calls=%async_computation.18 | async-start | bytes 15728640 | tf_op jit(solution)/shard_map/all_gather | solution.py:73
  668.8 540.1 %reduce-scatter.21.cloned.1.call-start = ((), (), s32[]{:S(2)}) async-start(), calls=%async_computation.19 | async-start | bytes 31457280 | tf_op jit(solution)/shard_map/reduce_scatter | solution.py:98
  974.5 359.3 %reduce-scatter.19.cloned.1.call-start = ((), (), s32[]{:S(2)}) async-start(), calls=%async_computation.17 | async-start | bytes 15728640 | tf_op jit(solution)/shard_map/reduce_scatter | solution.py:81
  1002.4 206.6 %copy-start.6 = (f32[2560]{0:T(1024)S(1)}, f32[2560]{0:T(1024)}, u32[]{:S(2)}) copy-start(f32[2560]{0:T(1024)} %copy-done.5) | copy-start | bytes 30724
  1002.4 206.6 %copy-start.10 = (f32[2560]{0:T(1024)S(1)}, f32[2560]{0:T(1024)}, u32[]{:S(2)}) copy-start(f32[2560]{0:T(1024)} %copy-done.9) | copy-start | bytes 30724
  1002.4 206.6 %copy-start.12 = (f32[1,1024]{1,0:T(1,128)S(1)}, f32[1,1024]{1,0:T(1,128)}, u32[]{:S(2)}) copy-start(f32[1,1024]{1,0:T(1,128)} %get-tuple-element.270) | copy-start | bytes 12292
  1002.4 206.6 %copy-start.19 = (f32[1,1024]{1,0:T(1,128)S(1)}, f32[1,1024]{1,0:T(1,128)}, u32[]{:S(2)}) copy-start(f32[1,1024]{1,0:T(1,128)} %get-tuple-element.273) | copy-start | bytes 12292
  1002.4 331.4 %copy-start.15 = (f32[2560]{0:T(1024)S(1)}, f32[2560]{0:T(1024)}, u32[]{:S(2)}) copy-start(f32[2560]{0:T(1024)} %copy-done.14) | copy-start | bytes 30724
  1002.4 331.4 %copy-start.25 = (f32[1,1024]{1,0:T(1,128)S(1)}, f32[1,1024]{1,0:T(1,128)}, u32[]{:S(2)}) copy-start(f32[1,1024]{1,0:T(1,128)} %get-tuple-element.268) | copy-start | bytes 12292
  1002.5 484.8 %all-gather.21.cloned.1.call-start = ((), (), s32[]{:S(2)}) async-start(), calls=%async_computation.20 | async-start | bytes 15728640 | tf_op jit(solution)/shard_map/all_gather | solution.py:73
  1357.6 598.0 %reduce-scatter.29.cloned.1.call-start = ((), (), s32[]{:S(2)}) async-start(), calls=%async_computation.24 | async-start | bytes 4456448 | tf_op jit(solution)/shard_map/reduce_scatter | solution.py:233
  1386.8 570.6 %reduce-scatter.27.cloned.1.call-start = ((), (), s32[]{:S(2)}) async-start(), calls=%async_computation.23 | async-start | bytes 4456448 | tf_op jit(solution)/shard_map/reduce_scatter | solution.py:230
  1386.8 100.4 %copy-start.33 = (bf16[512,1024]{0,1:T(8,128)(2,1)S(1)}, bf16[512,1024]{0,1:T(8,128)(2,1)}, u32[]{:S(2)}) copy-start(bf16[512,1024]{0,1:T(8,128)(2,1)} %all-gather.13.cloned.1.call-done) | copy-start | bytes 3145732
  1416.2 543.0 %reduce-scatter.31.cloned.1.call-start = ((), (), s32[]{:S(2)}) async-start(), calls=%async_computation.25 | async-start | bytes 139264
  1785.8 174.7 %all-reduce.4.cloned.1.call-start = ((), (), s32[]{:S(2)}) async-start(), calls=%async_computation.28 | async-start | bytes 8388608
  1814.1 202.2 %reduce-scatter.25.cloned.1.call-start = ((), (), s32[]{:S(2)}) async-start(), calls=%async_computation.22 | async-start | bytes 1114112 | tf_op jit(solution)/shard_map/reduce_scatter | solution.py:227
  1857.3 11.0 copy-start.2
  1868.3 383.6 %reduce-scatter.23.cloned.1.call-start = ((), (), s32[]{:S(2)}) async-start(), calls=%async_computation.21 | async-start | bytes 31457280 | tf_op jit(solution)/shard_map/reduce_scatter | solution.py:98
  1917.8 334.0 %copy-start.4 = (f32[2560]{0:T(1024)S(1)}, f32[2560]{0:T(1024)}, u32[]{:S(2)}) copy-start(f32[2560]{0:T(1024)} %copy-done.3) | copy-start | bytes 30724
  1917.8 334.0 %copy-start.8 = (f32[2560]{0:T(1024)S(1)}, f32[2560]{0:T(1024)}, u32[]{:S(2)}) copy-start(f32[2560]{0:T(1024)} %copy-done.7) | copy-start | bytes 30724
  1917.8 334.0 %copy-start.17 = (f32[1,1024]{1,0:T(1,128)S(1)}, f32[1,1024]{1,0:T(1,128)}, u32[]{:S(2)}) copy-start(f32[1,1024]{1,0:T(1,128)} %copy-done.16) | copy-start | bytes 12292
  1917.8 342.0 %copy-start.20 = (f32[1024]{0:T(1024)S(1)}, f32[1024]{0:T(1024)}, u32[]{:S(2)}) copy-start(f32[1024]{0:T(1024)} %get-tuple-element.215) | copy-start | bytes 12292
  1917.8 343.1 %copy-start.21 = (f32[1024]{0:T(1024)S(1)}, f32[1024]{0:T(1024)}, u32[]{:S(2)}) copy-start(f32[1024]{0:T(1024)} %get-tuple-element.222) | copy-start | bytes 12292
  1917.9 343.1 %copy-start.23 = (f32[1024]{0:T(1024)S(1)}, f32[1024]{0:T(1024)}, u32[]{:S(2)}) copy-start(f32[1024]{0:T(1024)} %get-tuple-element.257) | copy-start | bytes 12292
  1917.9 343.1 %copy-start.24 = (f32[1024]{0:T(1024)S(1)}, f32[1024]{0:T(1024)}, u32[]{:S(2)}) copy-start(f32[1024]{0:T(1024)} %get-tuple-element.267) | copy-start | bytes 12292
  1917.9 478.9 %reduce-scatter.33.cloned.1.call-start = ((), (), s32[]{:S(2)}) async-start(), calls=%async_computation.26 | async-start | bytes 540672
  2260.9 269.7 %reduce-scatter.35.cloned.1.call-start = ((), (), s32[]{:S(2)}) async-start(), calls=%async_computation.27 | async-start | bytes 540672
  (9 other events, 25.2 us)
Sparse Core Ops, SparseCore 0:
  10.2 48.2 all-gather.10
  177.2 35.8 all-gather.12
  512.2 117.9 reduce-scatter.16
  632.3 50.3 all-gather.14
  684.7 48.8 all-gather.16
  735.6 154.5 all-gather.18
  974.6 234.2 reduce-scatter.20
  1211.8 121.9 reduce-scatter.18
  1357.7 129.4 all-gather.20
  1490.9 72.9 reduce-scatter.28
  1567.8 71.5 reduce-scatter.26
  1785.9 55.8 reduce-scatter.30
  1845.5 110.4 all-reduce.3
  1959.5 56.7 reduce-scatter.24
  2018.5 233.3 reduce-scatter.22
  2261.1 135.7 reduce-scatter.32
  2398.9 131.6 reduce-scatter.34
